TPU v7x, 32 devices: a whole 2x2x4 slice. The times are simulated.
32 devices in a mesh: grp: 4 (over y, x), space: 8 (over z, core).
Axes of the slice: x: 2, y: 2, z: 4, core: 2. Of those that a mesh axis runs over, the one named last changes fastest.
Arguments:
- features: bfloat16 [4, 128, 128, 128], P('grp', 'space'), may hold values from -6 to 6
- weights: bfloat16 [27, 128, 128], replicated, may hold values from -0.109375 to 0.109375
- cotangent: bfloat16 [4, 128, 128, 128], P('grp', 'space'), may hold values from -6 to 6
- kernel_map: int32 [4, 128, 27], P('grp', 'space'), may hold values from -1 to 127, as said below
- counts: int32 [4, 8], P('grp', 'space'), may hold values from 4 to 16
Outputs:
- output: bfloat16 [4, 128, 128, 128], P('grp', 'space')
- input_grad: bfloat16 [4, 128, 128, 128], P('grp', 'space')
- weight_grad: float32 [3456, 128], P('space')
Inputs may be any that keep to these rules, and one draw needn't show every extreme that they name: `kernel_map`: the centre offset k = 27 div 2 maps every block to itself. Otherwise an entry for an output block b on slab d = b div 16 is -1 or lies in [d * 16 - 4, (d + 1) * 16 + 4) within the sample. The live blocks of a device are its first counts slots.
All inputs are finite; a program needn't handle non-finite values.
Results may differ from a plain program's by a relative error of at most 0.005.
Values may be sent and summed in bfloat16 or wider, within the bound.
A program may use at most 64 MiB of HBM per device.

v0:
```python
import jax
import jax.numpy as jnp
from jax import lax
from jax.sharding import PartitionSpec as P

K = 27
H = 4


def extended_2(block, sides, width):
    for axis, dim in sides:
        count = lax.axis_size(axis)
        forward = [(i, i + 1) for i in range(count - 1)]
        backward = [(target, source) for source, target in forward]
        low = lax.ppermute(
            lax.slice_in_dim(block, block.shape[dim] - width, None, axis=dim), axis, forward
        )
        high = lax.ppermute(lax.slice_in_dim(block, 0, width, axis=dim), axis, backward)
        block = jnp.concatenate([low, block, high], axis=dim)
    return block


def passed_along(block, axis, distance):
    devices = range(lax.axis_size(axis))
    route = [(i - distance, i) for i in devices if i - distance in devices]
    return lax.ppermute(block, axis, route)


def per_device(features, weights, cotangent, kernel_map, counts):
    voxels = features[0]
    slots = voxels.shape[0]
    device = lax.axis_index("space")
    live_mask = (jnp.arange(slots) < counts[0, 0]).astype(jnp.bfloat16)[:, None, None]
    live_float = live_mask.astype(jnp.float32)
    masked = voxels * live_mask
    grad_out = cotangent[0] * live_mask
    extended = extended_2(masked, (("space", 0),), H)
    block_map = kernel_map[0]
    first_block = device * slots - H
    present = (block_map >= 0).astype(jnp.bfloat16)
    local_index = jnp.where(block_map >= 0, block_map - first_block, 0)
    channels_in = voxels.shape[2]
    channels_out = weights.shape[2]

    def step(offset, carry):
        total, grad_in, wgrad = carry
        column = lax.dynamic_index_in_dim(local_index, offset, 1, keepdims=False)
        present_k = lax.dynamic_index_in_dim(present, offset, 1, keepdims=False)[:, None, None]
        gathered = jnp.take(extended, column, axis=0) * present_k
        kernel = lax.dynamic_index_in_dim(weights, offset, 0, keepdims=False)
        total = total + jnp.einsum(
            "brc,co->bro", gathered, kernel, preferred_element_type=jnp.float32
        )
        term = jnp.einsum("bro,co->brc", grad_out, kernel, preferred_element_type=jnp.float32)
        grad_in = grad_in.at[column].add(term * present_k.astype(jnp.float32))
        piece = jnp.einsum("brc,bro->co", gathered, grad_out, preferred_element_type=jnp.float32)
        wgrad = lax.dynamic_update_index_in_dim(wgrad, piece, offset, 0)
        return (total, grad_in, wgrad)

    start = (
        jnp.zeros((slots, voxels.shape[1], channels_out), jnp.float32),
        jnp.zeros((slots + 2 * H, voxels.shape[1], channels_in), jnp.float32),
        jnp.zeros((K, channels_in, channels_out), jnp.float32),
    )
    total, grad_in, wgrad = lax.fori_loop(0, K, step, start)
    output = (total * live_float).astype(jnp.bfloat16)
    lower_rim = grad_in[:H]
    upper_rim = grad_in[slots + H :]
    own_grad = grad_in[H : slots + H]
    from_above = passed_along(lower_rim.astype(jnp.bfloat16), "space", -1).astype(lower_rim.dtype)
    from_below = passed_along(upper_rim.astype(jnp.bfloat16), "space", 1).astype(upper_rim.dtype)
    own_grad = own_grad.at[:H].add(from_below)
    own_grad = own_grad.at[slots - H :].add(from_above)
    input_grad = (own_grad * live_float).astype(jnp.bfloat16)
    weight_rows = wgrad.reshape(K * channels_in, channels_out)
    summed = lax.psum(weight_rows, ("grp", "space"))
    row_count = weight_rows.shape[0] // lax.axis_size("space")
    own_rows = lax.dynamic_slice_in_dim(summed, device * row_count, row_count, 0)
    return (output[None], input_grad[None], own_rows)


def solution(mesh):
    in_specs = (
        P("grp", "space", None, None),
        P(),
        P("grp", "space", None, None),
        P("grp", "space", None),
        P("grp", "space"),
    )
    out_specs = (P("grp", "space", None, None), P("grp", "space", None, None), P("space", None))
    return jax.shard_map(
        per_device, mesh=mesh, in_specs=in_specs, out_specs=out_specs, check_vma=False
    )
```

profile of v0, /device:TPU:0, one launch (start us, length us, event | category | flops | bytes accessed | tf_op | source)
XLA Modules:
  0.0 446.6 jit_solution(6604111132095993957)
XLA Ops:
  13.1 4.0 collective-permute-done.1
  19.4 278.4 %while.20 = (s32[]{:T(128)}, f32[16,128,128]{2,1,0:T(8,128)}, f32[24,128,128]{2,1,0:T(8,128)}, f32[27,128,128]{2,1,0:T(8,128)}, s32[16,27]{0,1:T(8,128)S(1)}, /*...) while((s32[]{:T(128)}, f32[16,128,128]{2,1,0:T(8,128)}, ...), condition=%wide.region_2.3_spmd.clone, body=%wide.region_0.2_spmd.clone.sunk | while | flops 203424880 | bytes 11670275 | solution.py:65
  24.7 3.5 scatter_fusion
  35.2 3.4 scatter_fusion
  45.6 3.3 scatter_fusion
  55.9 3.4 scatter_fusion
  97.1 3.4 scatter_fusion
  107.5 3.3 scatter_fusion
  117.8 3.3 scatter_fusion
  138.3 3.4 scatter_fusion
  158.9 3.4 scatter_fusion
  179.6 3.4 scatter_fusion
  189.9 3.4 scatter_fusion
  200.3 3.4 scatter_fusion
  210.6 3.4 scatter_fusion
  220.9 3.4 scatter_fusion
  231.2 3.4 scatter_fusion
  241.6 3.3 scatter_fusion
  251.9 3.4 scatter_fusion
  262.3 3.3 scatter_fusion
  272.6 3.4 scatter_fusion
  293.2 3.4 scatter_fusion
  299.4 6.2 %collective-permute-start.2 = (bf16[4,128,128]{2,1,0:T(8,128)(2,1)S(1)}, bf16[4,128,128]{2,1,0:T(8,128)(2,1)S(1)}, u32[]{:S(2)}, u32[]{:S(2)}) collective-permute-start(bf16[4,128,128]{2,1,0:T(8,128)(2,1)S(1)} %get-tuple-element.239), channel_id=1, source_target_pairs={{0,1},{1,2},{2,3},{3,4},{4,5},{5,6},{6,7},{8,9},{9,10},{10,11},{11... | collective-permute-start | bytes 393224 | tf_op jit(solution)/shard_map/ppermute | solution.py:26
  311.6 126.6 %all-reduce.2.cloned.1.call-done = f32[3456,128]{1,0:T(8,128)} async-done(((f32[3456,128]{1,0:T(8,128)}), f32[3456,128]{1,0:T(8,128)}) %all-reduce.2.cloned.1.call-update) | async-done | bytes 1769488 | tf_op jit(solution)/shard_map/psum | solution.py:76
  (253 shorter events, 226.5 us)
Async XLA Ops:
  7.2 5.8 %copy-start.1 = (s32[1,16,27]{2,1,0:T(8,128)S(1)}, s32[1,16,27]{2,1,0:T(8,128)}, u32[]{:S(2)}) copy-start(s32[1,16,27]{2,1,0:T(8,128)} %param.14) | copy-start | bytes 5188
  7.2 431.0 %all-reduce.2.cloned.1.call-start = ((), (), s32[]{:S(2)}) async-start(), calls=%async_computation | async-start | bytes 3538944 | tf_op jit(solution)/shard_map/psum | solution.py:76
  9.2 3.8 collective-permute-start
  11.7 5.4 %collective-permute-start.1 = (bf16[4,128,128]{2,1,0:T(8,128)(2,1)S(1)}, bf16[4,128,128]{2,1,0:T(8,128)(2,1)S(1)}, u32[]{:S(2)}, u32[]{:S(2)}) collective-permute-start(bf16[4,128,128]{2,1,0:T(8,128)(2,1)S(1)} %get-tuple-element.241), channel_id=1, source_target_pairs={{1,0},{2,1},{3,2},{4,3},{5,4},{6,5},{7,6},{9,8},{10,9},{11,10},{12... | collective-permute-start | bytes 393224 | tf_op jit(solution)/shard_map/ppermute | solution.py:18
  297.7 7.9 %copy-start = (f32[24,128,128]{2,1,0:T(8,128)S(1)}, f32[24,128,128]{2,1,0:T(8,128)}, u32[]{:S(2)}) copy-start(f32[24,128,128]{2,1,0:T(8,128)} %get-tuple-element.184) | copy-start | bytes 4718596
  299.4 7.6 %collective-permute-start.2 = (bf16[4,128,128]{2,1,0:T(8,128)(2,1)S(1)}, bf16[4,128,128]{2,1,0:T(8,128)(2,1)S(1)}, u32[]{:S(2)}, u32[]{:S(2)}) collective-permute-start(bf16[4,128,128]{2,1,0:T(8,128)(2,1)S(1)} %get-tuple-element.239), channel_id=1, source_target_pairs={{0,1},{1,2},{2,3},{3,4},{4,5},{5,6},{6,7},{8,9},{9,10},{10,11},{11... | collective-permute-start | bytes 393224 | tf_op jit(solution)/shard_map/ppermute | solution.py:26
  305.8 3.2 collective-permute-start.3
Sparse Core Ops, SparseCore 0:
  305.8 132.3 all-reduce.1
where the time goes:
time: 453 us; the launch traced here: 447 us
  waiting for transfers between devices  132 us (29%)
  matrix products  129 us (28%)
  other arithmetic  98.1 us (22%)
  local copies, waits for them, and re-layouts  60.2 us (13%)
  between operations  14.8 us (3%)
  starting transfers between devices  11.2 us (2%)
    psum x1, waiting for transfers between devices, per_device(): summed = lax.psum(weight_rows, ('grp', 'space'))  127 us
    scatter-add x27, other arithmetic, step(): grad_in = grad_in.at[column].add(term * present_k.astype(jnp.float32))  90.8 us
    dot_general x27, matrix products, step(): jnp.einsum('brc,co->bro', gathered, kernel, preferred_element_type=jnp.fl...  70 us
    gather x27, local copies, waits for them, and re-layouts, step(): gathered = jnp.take(extended, column, axis=0) * present_k  48.1 us
    dot_general x27, matrix products, step(): jnp.einsum('brc,bro->co', gathered, grad_out, preferred_element_type=jnp....  30.5 us
    dot_general x27, matrix products, step(): jnp.einsum('bro,co->brc', grad_out, kernel, preferred_element_type=jnp.fl...  28.4 us
  transfers between devices with their start and end apart: 5, of which 3 were waited for; matrix products, arithmetic and copies ran while one was open for 1% of the time, Pallas kernels for 0%

commit v1 on v0

--- a/solution.py
+++ b/solution.py
@@ -2,6 +2,7 @@
 import jax.numpy as jnp
 from jax import lax
 from jax.sharding import PartitionSpec as P
+from jax.lax import psum
 
 K = 27
 H = 4
@@ -73,7 +74,8 @@
     own_grad = own_grad.at[slots - H :].add(from_above)
     input_grad = (own_grad * live_float).astype(jnp.bfloat16)
     weight_rows = wgrad.reshape(K * channels_in, channels_out)
-    summed = lax.psum(weight_rows, ("grp", "space"))
+    after = psum(weight_rows, "grp")
+    summed = psum(after, "space")
     row_count = weight_rows.shape[0] // lax.axis_size("space")
     own_rows = lax.dynamic_slice_in_dim(summed, device * row_count, row_count, 0)
     return (output[None], input_grad[None], own_rows)

time: 453 us -> 446 us (0.985)
  waiting for transfers between devices: 132 us -> 126 us
    psum x1 -> x2, waiting for transfers between devices: 127 us -> 120 us  [the longest x1 60 us: per_device(): after = psum(weight_rows, 'grp')]
  transfers between devices with their start and end apart: 5 -> 6, of which waited for: 3 -> 4; matrix products, arithmetic and copies ran while one was open for 1% -> 1% of each run, Pallas kernels for 0% -> 0%
where the time goes in v1:
time: 446 us; the launch traced here: 440 us
  matrix products  129 us (29%)
  waiting for transfers between devices  126 us (28%)
  other arithmetic  96.6 us (22%)
  local copies, waits for them, and re-layouts  61.5 us (14%)
  between operations  14.8 us (3%)
  starting transfers between devices  11.2 us (3%)
    scatter-add x27, other arithmetic, step(): grad_in = grad_in.at[column].add(term * present_k.astype(jnp.float32))  90.8 us
    dot_general x27, matrix products, step(): jnp.einsum('brc,co->bro', gathered, kernel, preferred_element_type=jnp.fl...  70 us
    psum x1, waiting for transfers between devices, per_device(): after = psum(weight_rows, 'grp')  60 us
    psum x1, waiting for transfers between devices, per_device(): summed = psum(after, 'space')  59.8 us
    gather x27, local copies, waits for them, and re-layouts, step(): gathered = jnp.take(extended, column, axis=0) * present_k  48.1 us
    dot_general x27, matrix products, step(): jnp.einsum('brc,bro->co', gathered, grad_out, preferred_element_type=jnp....  30.5 us
    dot_general x27, matrix products, step(): jnp.einsum('bro,co->brc', grad_out, kernel, preferred_element_type=jnp.fl...  28.4 us
    mul x27, local copies, waits for them, and re-layouts, step(): grad_in = grad_in.at[column].add(term * present_k.astype(jnp.float32))  8.94 us
  transfers between devices with their start and end apart: 6, of which 4 were waited for; matrix products, arithmetic and copies ran while one was open for 1% of the time, Pallas kernels for 0%

profile of v1, /device:TPU:0, one launch (start us, length us, event | category | flops | bytes accessed | tf_op | source)
XLA Modules:
  0.0 439.6 jit_solution(15036566858600868694)
XLA Ops:
  13.1 4.0 collective-permute-done.1
  19.4 278.4 %while.20 = (s32[]{:T(128)}, f32[16,128,128]{2,1,0:T(8,128)}, f32[24,128,128]{2,1,0:T(8,128)}, f32[27,128,128]{2,1,0:T(8,128)}, s32[16,27]{0,1:T(8,128)S(1)}, /*...) while((s32[]{:T(128)}, f32[16,128,128]{2,1,0:T(8,128)}, ...), condition=%wide.region_2.3_spmd.clone, body=%wide.region_0.2_spmd.clone.sunk | while | flops 203424880 | bytes 11670275 | solution.py:66
  24.7 3.5 scatter_fusion
  35.2 3.4 scatter_fusion
  45.6 3.3 scatter_fusion
  55.9 3.4 scatter_fusion
  97.1 3.4 scatter_fusion
  107.5 3.3 scatter_fusion
  117.8 3.3 scatter_fusion
  138.3 3.4 scatter_fusion
  158.9 3.4 scatter_fusion
  179.6 3.4 scatter_fusion
  189.9 3.4 scatter_fusion
  200.3 3.4 scatter_fusion
  210.6 3.4 scatter_fusion
  220.9 3.4 scatter_fusion
  231.2 3.4 scatter_fusion
  251.9 3.4 scatter_fusion
  262.3 3.3 scatter_fusion
  272.6 3.4 scatter_fusion
  293.2 3.4 scatter_fusion
  299.3 6.2 %collective-permute-start.2 = (bf16[4,128,128]{2,1,0:T(8,128)(2,1)S(1)}, bf16[4,128,128]{2,1,0:T(8,128)(2,1)S(1)}, u32[]{:S(2)}, u32[]{:S(2)}) collective-permute-start(bf16[4,128,128]{2,1,0:T(8,128)(2,1)S(1)} %get-tuple-element.239), channel_id=1, source_target_pairs={{0,1},{1,2},{2,3},{3,4},{4,5},{5,6},{6,7},{8,9},{9,10},{10,11},{11... | collective-permute-start | bytes 393224 | tf_op jit(solution)/shard_map/ppermute | solution.py:27
  305.5 60.0 %all-reduce.3.cloned.1.call-done = f32[3456,128]{1,0:T(8,128)} async-done(((f32[3456,128]{1,0:T(8,128)}), f32[3456,128]{1,0:T(8,128)}) %all-reduce.3.cloned.1.call-update) | async-done | bytes 1769488 | tf_op jit(solution)/shard_map/psum | solution.py:77
  371.4 59.8 %all-reduce.5.cloned.1.call-done = f32[3456,128]{1,0:T(8,128)} async-done(((f32[3456,128]{1,0:T(8,128)}), f32[3456,128]{1,0:T(8,128)}) %all-reduce.5.cloned.1.call-update) | async-done | bytes 1769488 | tf_op jit(solution)/shard_map/psum | solution.py:78
  (256 shorter events, 229.7 us)
Async XLA Ops:
  7.2 5.8 %copy-start.1 = (s32[1,16,27]{2,1,0:T(8,128)S(1)}, s32[1,16,27]{2,1,0:T(8,128)}, u32[]{:S(2)}) copy-start(s32[1,16,27]{2,1,0:T(8,128)} %param.14) | copy-start | bytes 5188
  7.2 358.3 %all-reduce.3.cloned.1.call-start = ((), (), s32[]{:S(2)}) async-start(), calls=%async_computation | async-start | bytes 3538944 | tf_op jit(solution)/shard_map/psum | solution.py:77
  9.2 3.8 collective-permute-start
  11.7 5.4 %collective-permute-start.1 = (bf16[4,128,128]{2,1,0:T(8,128)(2,1)S(1)}, bf16[4,128,128]{2,1,0:T(8,128)(2,1)S(1)}, u32[]{:S(2)}, u32[]{:S(2)}) collective-permute-start(bf16[4,128,128]{2,1,0:T(8,128)(2,1)S(1)} %get-tuple-element.241), channel_id=1, source_target_pairs={{1,0},{2,1},{3,2},{4,3},{5,4},{6,5},{7,6},{9,8},{10,9},{11,10},{12... | collective-permute-start | bytes 393224 | tf_op jit(solution)/shard_map/ppermute | solution.py:19
  297.7 1.4 copy-start
  297.8 133.4 %all-reduce.5.cloned.1.call-start = ((), (), s32[]{:S(2)}) async-start(), calls=%async_computation.1 | async-start | bytes 3538944 | tf_op jit(solution)/shard_map/psum | solution.py:78
  299.3 67.6 %collective-permute-start.2 = (bf16[4,128,128]{2,1,0:T(8,128)(2,1)S(1)}, bf16[4,128,128]{2,1,0:T(8,128)(2,1)S(1)}, u32[]{:S(2)}, u32[]{:S(2)}) collective-permute-start(bf16[4,128,128]{2,1,0:T(8,128)(2,1)S(1)} %get-tuple-element.239), channel_id=1, source_target_pairs={{0,1},{1,2},{2,3},{3,4},{4,5},{5,6},{6,7},{8,9},{9,10},{10,11},{11... | collective-permute-start | bytes 393224 | tf_op jit(solution)/shard_map/ppermute | solution.py:27
  365.6 3.2 collective-permute-start.3
Sparse Core Ops, SparseCore 0:
  297.9 67.5 all-reduce.2
  367.8 63.2 all-reduce.4
